TPU v7x, 256 devices: a whole 4x4x8 slice. The times are simulated.
256 devices in a mesh: gx: 32 (over z, x), gy: 8 (over y, core).
Axes of the slice: x: 4, y: 4, z: 8, core: 2. Of those that a mesh axis runs over, the one named last changes fastest.
Arguments:
- right_side: float32 [8192, 512], P(('gx', 'gy')), may hold values from -6 to 6
- diagonal: float32 [8192, 512], P(('gx', 'gy')), may hold values from 0.5 to 2
- features: float32 [8192, 64, 512], P(('gx', 'gy')), may hold values from -0.078125 to 0.078125
- neighbours: int32 [8192, 27], P(('gx', 'gy')), may hold values from -1 to 8191, as said below
- vertex_features: float32 [64, 262144], P(None, ('gx', 'gy')), may hold values from -0.75 to 0.75
- vertex_bricks: int32 [262144], P(('gx', 'gy')), may hold values from 0 to 8191, as said below
Outputs:
- solution_field: float32 [8192, 512], P(('gx', 'gy'))
- residual: float32 [8192, 512], P(('gx', 'gy'))
- vertex_values: float32 [262144], P(('gx', 'gy'))
Inputs may be any that keep to these rules, and one draw needn't show every extreme that they name: `neighbours`: bricks sit at distinct integer brick coordinates; slot k of a row names the brick at the offset (k // 9 - 1, k // 3 % 3 - 1, k % 3 - 1) from its own, or -1 where no brick is there, so slot 13 names the brick itself and the relation is symmetric. Every brick whose coordinates differ from a brick's by at most two in each direction is held by a device whose gx and gy indices each differ from that brick's holder's by at most one. `vertex_bricks`: vertex n names a brick of its own gx slab: a brick from (n // 8192) * 256 to (n // 8192) * 256 + 255.
All inputs are finite; a program needn't handle non-finite values.
Results may differ from a plain program's by a relative error of at most 0.0002.
Values sent between devices are 32-bit elements; how exact they have to be, the bound alone decides.
No kernel may reach another device: no remote copies, remote signals or barrier semaphores. Data moves between devices by JAX's collectives and lax.ppermute only.
A program may use at most 64 MiB of HBM per device.

v0:
```python
import jax
import jax.numpy as jnp
from jax import lax
from jax.sharding import PartitionSpec as P

ITERS = 3


def with_halo(cells, sides, width):
    for axis, dim in sides:
        count = lax.axis_size(axis)
        ends = count - 1
        head = lax.slice_in_dim(cells, 0, width, axis=dim)
        tail = lax.slice_in_dim(cells, cells.shape[dim] - width, cells.shape[dim], axis=dim)
        cells = jnp.concatenate(
            [
                lax.ppermute(tail, axis, [(i, (i + 1) % count) for i in range(ends)]),
                cells,
                lax.ppermute(head, axis, [((i + 1) % count, i) for i in range(ends)]),
            ],
            axis=dim,
        )
    return cells


def coefficient(features, field):
    return jnp.einsum("bfv,bv->bf", features, field, precision=lax.Precision.HIGHEST)


def squares(values):
    return lax.psum(jnp.sum(values * values), ("gx", "gy"))


def per_device(right_side, diagonal, features, neighbours, vertex_features, vertex_bricks):
    nrows = features.shape[0]
    width = features.shape[1]
    across = lax.axis_size("gy")
    row_index = lax.axis_index("gx")
    col_index = lax.axis_index("gy")
    targets = jnp.arange(9 * nrows, dtype=jnp.int32)
    valid = neighbours >= 0
    safe_ids = jnp.where(valid, neighbours, 0)
    owner = safe_ids // nrows
    offset_x = owner // across - row_index + 1
    offset_y = owner % across - col_index + 1
    inside = valid & (offset_x >= 0) & (offset_x < 3) & (offset_y >= 0) & (offset_y < 3)
    position, inside = ((offset_x * 3 + offset_y) * nrows + safe_ids % nrows, inside)
    hits = (position[:, :, None] == targets[None, None, :]) & inside[:, :, None]
    counts = jnp.sum(hits.astype(jnp.float32), axis=1)

    def first_halo(values):
        cycle = with_halo(values.reshape(1, 1, nrows, width), (("gx", 0), ("gy", 1)), 1)
        return cycle.reshape(9 * nrows, width)

    def first_sum(values):
        return jnp.dot(counts, first_halo(values), precision=lax.Precision.HIGHEST)

    solution_field = jnp.zeros_like(right_side)
    residual = right_side
    direction = right_side
    norm_now = squares(residual)
    for step in range(ITERS):
        second_cycle = with_halo(
            first_sum(coefficient(features, direction)).reshape(1, 1, nrows, width),
            (("gx", 0), ("gy", 1)),
            1,
        )
        second = jnp.dot(
            counts, second_cycle.reshape(9 * nrows, width), precision=lax.Precision.HIGHEST
        )
        image = diagonal * direction + jnp.einsum(
            "bfv,bf->bv", features, second, precision=lax.Precision.HIGHEST
        )
        alpha = norm_now / lax.psum(jnp.sum(direction * image), ("gx", "gy"))
        solution_field = solution_field + alpha * direction
        residual = residual - alpha * image
        norm_next = squares(residual)
        direction = residual + norm_next / norm_now * direction
        norm_now = norm_next
    surface = first_sum(coefficient(features, solution_field))
    slab_rows = lax.all_gather(surface, "gy", axis=0, tiled=True)
    local_ids = vertex_bricks - row_index * across * nrows
    picked = jnp.take(slab_rows, local_ids, axis=0)
    vertex_values = jnp.sum(vertex_features * picked.T, axis=0)
    return (solution_field, residual, vertex_values)


def solution(mesh):
    placed = (
        P(("gx", "gy"), None),
        P(("gx", "gy"), None),
        P(("gx", "gy"), None, None),
        P(("gx", "gy"), None),
        P(None, ("gx", "gy")),
        P(("gx", "gy")),
    )
    return jax.shard_map(
        per_device,
        mesh=mesh,
        in_specs=placed,
        out_specs=(P(("gx", "gy"), None), P(("gx", "gy"), None), P(("gx", "gy"))),
        check_vma=False,
    )
```

profile of v0, /device:TPU:129, one launch (start us, length us, event | category | flops | bytes accessed | tf_op | source)
XLA Modules:
  0.0 560.7 jit_solution(662496368784365687)
XLA Ops:
  0.7 5.8 %fusion.8 = f32[32,1,64]{2,1,0:T(1,128)S(1)} fusion(f32[32,64,512]{2,1,0:T(8,128)} %param.8, f32[32,512,1]{1,0,2:T(8,128)} %bitcast.92), kind=kOutput, calls=%fused_computation.25 | convolution fusion | flops 12582912 | bytes 4268032 | tf_op jit(solution)/shard_map/bfv,bv->bf/dot_general | solution.py:27
  12.7 5.6 collective-permute-done
  18.2 4.0 collective-permute-start.3
  32.1 4.4 collective-permute-done.4
  38.6 5.2 collective-permute-start.6
  45.2 4.3 fusion.25
  50.2 74.5 %all-reduce = (f32[]{:T(128)}, f32[]{:T(128)}) all-reduce(f32[]{:T(128)} %get-tuple-element.4, f32[]{:T(128)} %get-tuple-element.3), channel_id=1, replica_groups=mesh['gx'=32,'gy'=8] {'gx','gy'}, use_global_device_ids=true, to_apply=%region_1.2 | all-reduce | flops 2 | bytes 16 | tf_op jit(solution)/shard_map/psum | solution.py:31
  126.7 73.5 %psum.44 = f32[]{:T(128)} all-reduce(f32[]{:T(128)} %get-tuple-element.9), channel_id=1, replica_groups=mesh['gx'=32,'gy'=8] {'gx','gy'}, use_global_device_ids=true, to_apply=%region_6.7 | all-reduce | flops 1 | bytes 8 | tf_op jit(solution)/shard_map/psum | solution.py:31
  201.5 5.4 fusion.6
  212.7 5.9 %collective-permute-done.8 = f32[1,1,32,64]{3,2,1,0:T(8,128)S(1)} collective-permute-done((f32[1,1,32,64]{3,2,1,0:T(8,128)S(1)}, f32[1,1,32,64]{3,2,1,0:T(8,128)S(1)}, u32[]{:S(2)}, u32[]{:S(2)}) %collective-permute-start.8) | collective-permute-done | bytes 8224 | tf_op jit(solution)/shard_map/ppermute | solution.py:17
  218.6 4.0 collective-permute-start.11
  231.3 4.4 collective-permute-done.12
  238.9 4.3 collective-permute-start.14
  247.1 73.2 %psum.45 = f32[]{:T(128)} all-reduce(f32[]{:T(128)} %multiply_reduce_fusion.2), channel_id=1, replica_groups=mesh['gx'=32,'gy'=8] {'gx','gy'}, use_global_device_ids=true, to_apply=%region_8.9 | all-reduce | flops 1 | bytes 8 | tf_op jit(solution)/shard_map/psum | solution.py:74
  322.3 73.3 %psum.46 = f32[]{:T(128)} all-reduce(f32[]{:T(128)} %get-tuple-element.7), channel_id=1, replica_groups=mesh['gx'=32,'gy'=8] {'gx','gy'}, use_global_device_ids=true, to_apply=%region_10.11 | all-reduce | flops 1 | bytes 8 | tf_op jit(solution)/shard_map/psum | solution.py:31
  397.0 5.4 fusion.4
  402.4 4.2 collective-permute-start.17
  408.6 5.9 %collective-permute-done.16 = f32[1,1,32,64]{3,2,1,0:T(8,128)S(1)} collective-permute-done((f32[1,1,32,64]{3,2,1,0:T(8,128)S(1)}, f32[1,1,32,64]{3,2,1,0:T(8,128)S(1)}, u32[]{:S(2)}, u32[]{:S(2)}) %collective-permute-start.16) | collective-permute-done | bytes 8224 | tf_op jit(solution)/shard_map/ppermute | solution.py:17
  427.1 4.4 collective-permute-done.20
  434.8 4.1 collective-permute-start.22
  443.0 73.2 %psum.47 = f32[]{:T(128)} all-reduce(f32[]{:T(128)} %multiply_reduce_fusion), channel_id=1, replica_groups=mesh['gx'=32,'gy'=8] {'gx','gy'}, use_global_device_ids=true, to_apply=%region_12.13 | all-reduce | flops 1 | bytes 8 | tf_op jit(solution)/shard_map/psum | solution.py:74
  518.2 5.3 fusion.2
  529.2 5.8 %collective-permute-done.24 = f32[1,1,32,64]{3,2,1,0:T(8,128)S(1)} collective-permute-done((f32[1,1,32,64]{3,2,1,0:T(8,128)S(1)}, f32[1,1,32,64]{3,2,1,0:T(8,128)S(1)}, u32[]{:S(2)}, u32[]{:S(2)}) %collective-permute-start.24) | collective-permute-done | bytes 8224 | tf_op jit(solution)/shard_map/ppermute | solution.py:17
  543.8 13.1 %all_gather.3 = f32[256,64]{1,0:T(8,128)S(1)} all-gather(f32[32,64]{1,0:T(8,128)S(1)} %fusion.30), channel_id=1, replica_groups=mesh['gx'=32,'gy'=8] {'gy'}, dimensions={0}, use_global_device_ids=true | all-gather | bytes 73728 | tf_op jit(solution)/shard_map/all_gather | solution.py:81
  (100 shorter events, 83.5 us)
Async XLA Ops:
  6.5 6.2 %collective-permute-start.1 = (f32[1,1,32,64]{3,2,1,0:T(8,128)S(1)}, f32[1,1,32,64]{3,2,1,0:T(8,128)S(1)}, u32[]{:S(2)}, u32[]{:S(2)}) collective-permute-start(f32[1,1,32,64]{3,2,1,0:T(8,128)S(1)} %bitcast.101), channel_id=1, source_target_pairs={{8,0},{16,8},{24,16},{32,24},{40,32},{48,40},{56,48},{64,56},{72,6... | collective-permute-start | bytes 24584 | tf_op jit(solution)/shard_map/ppermute | solution.py:19
  10.4 7.8 %collective-permute-start = (f32[1,1,32,64]{3,2,1,0:T(8,128)S(1)}, f32[1,1,32,64]{3,2,1,0:T(8,128)S(1)}, u32[]{:S(2)}, u32[]{:S(2)}) collective-permute-start(f32[1,1,32,64]{3,2,1,0:T(8,128)S(1)} %bitcast.102), channel_id=1, source_target_pairs={{0,8},{8,16},{16,24},{24,32},{32,40},{40,48},{48,56},{56,64},{64,7... | collective-permute-start | bytes 24584 | tf_op jit(solution)/shard_map/ppermute | solution.py:17
  18.2 7.4 %collective-permute-start.3 = (f32[3,1,32,64]{3,2,1,0:T(8,128)S(1)}, f32[3,1,32,64]{3,2,1,0:T(8,128)S(1)}, u32[]{:S(2)}, u32[]{:S(2)}) collective-permute-start(f32[3,1,32,64]{3,2,1,0:T(8,128)S(1)} %pad_maximum_fusion.7), channel_id=1, source_target_pairs={{1,0},{2,1},{3,2},{4,3},{5,4},{6,5},{7,6},{9,8},{10,9},{11,10},{12... | collective-permute-start | bytes 73736 | tf_op jit(solution)/shard_map/ppermute | solution.py:19
  26.8 5.3 collective-permute-start.5
  28.7 7.8 %collective-permute-start.4 = (f32[1,1,32,64]{3,2,1,0:T(8,128)S(1)}, f32[1,1,32,64]{3,2,1,0:T(8,128)S(1)}, u32[]{:S(2)}, u32[]{:S(2)}) collective-permute-start(f32[1,1,32,64]{3,2,1,0:T(8,128)S(1)} %convolution_bitcast_fusion.2), channel_id=1, source_target_pairs={{0,8},{8,16},{16,24},{24,32},{32,40},{40,48},{48,56},{56,64},{64,7... | collective-permute-start | bytes 24584 | tf_op jit(solution)/shard_map/ppermute | solution.py:17
  36.5 7.3 %collective-permute-start.7 = (f32[3,1,32,64]{3,2,1,0:T(8,128)S(1)}, f32[3,1,32,64]{3,2,1,0:T(8,128)S(1)}, u32[]{:S(2)}, u32[]{:S(2)}) collective-permute-start(f32[3,1,32,64]{3,2,1,0:T(8,128)S(1)} %pad_maximum_fusion.8), channel_id=1, source_target_pairs={{1,0},{2,1},{3,2},{4,3},{5,4},{6,5},{7,6},{9,8},{10,9},{11,10},{12... | collective-permute-start | bytes 73736 | tf_op jit(solution)/shard_map/ppermute | solution.py:19
  38.6 6.4 %collective-permute-start.6 = (f32[3,1,32,64]{3,2,1,0:T(8,128)S(1)}, f32[3,1,32,64]{3,2,1,0:T(8,128)S(1)}, u32[]{:S(2)}, u32[]{:S(2)}) collective-permute-start(f32[3,1,32,64]{3,2,1,0:T(8,128)S(1)} %pad_maximum_fusion.8), channel_id=1, source_target_pairs={{0,1},{1,2},{2,3},{3,4},{4,5},{5,6},{6,7},{8,9},{9,10},{10,11},{11... | collective-permute-start | bytes 73736 | tf_op jit(solution)/shard_map/ppermute | solution.py:17
  206.9 5.8 %collective-permute-start.9 = (f32[1,1,32,64]{3,2,1,0:T(8,128)S(1)}, f32[1,1,32,64]{3,2,1,0:T(8,128)S(1)}, u32[]{:S(2)}, u32[]{:S(2)}) collective-permute-start(f32[1,1,32,64]{3,2,1,0:T(8,128)S(1)} %bitcast.113), channel_id=1, source_target_pairs={{8,0},{16,8},{24,16},{32,24},{40,32},{48,40},{56,48},{64,56},{72,6... | collective-permute-start | bytes 24584 | tf_op jit(solution)/shard_map/ppermute | solution.py:19
  210.8 7.8 %collective-permute-start.8 = (f32[1,1,32,64]{3,2,1,0:T(8,128)S(1)}, f32[1,1,32,64]{3,2,1,0:T(8,128)S(1)}, u32[]{:S(2)}, u32[]{:S(2)}) collective-permute-start(f32[1,1,32,64]{3,2,1,0:T(8,128)S(1)} %bitcast.114), channel_id=1, source_target_pairs={{0,8},{8,16},{16,24},{24,32},{32,40},{40,48},{48,56},{56,64},{64,7... | collective-permute-start | bytes 24584 | tf_op jit(solution)/shard_map/ppermute | solution.py:17
  218.6 5.9 %collective-permute-start.11 = (f32[3,1,32,64]{3,2,1,0:T(8,128)S(1)}, f32[3,1,32,64]{3,2,1,0:T(8,128)S(1)}, u32[]{:S(2)}, u32[]{:S(2)}) collective-permute-start(f32[3,1,32,64]{3,2,1,0:T(8,128)S(1)} %pad_maximum_fusion.9), channel_id=1, source_target_pairs={{1,0},{2,1},{3,2},{4,3},{5,4},{6,5},{7,6},{9,8},{10,9},{11,10},{12... | collective-permute-start | bytes 73736 | tf_op jit(solution)/shard_map/ppermute | solution.py:19
  226.0 5.3 collective-permute-start.13
  227.9 7.8 %collective-permute-start.12 = (f32[1,1,32,64]{3,2,1,0:T(8,128)S(1)}, f32[1,1,32,64]{3,2,1,0:T(8,128)S(1)}, u32[]{:S(2)}, u32[]{:S(2)}) collective-permute-start(f32[1,1,32,64]{3,2,1,0:T(8,128)S(1)} %convolution_bitcast_fusion.1), channel_id=1, source_target_pairs={{0,8},{8,16},{16,24},{24,32},{32,40},{40,48},{48,56},{56,64},{64,7... | collective-permute-start | bytes 24584 | tf_op jit(solution)/shard_map/ppermute | solution.py:17
  235.7 7.5 %collective-permute-start.15 = (f32[3,1,32,64]{3,2,1,0:T(8,128)S(1)}, f32[3,1,32,64]{3,2,1,0:T(8,128)S(1)}, u32[]{:S(2)}, u32[]{:S(2)}) collective-permute-start(f32[3,1,32,64]{3,2,1,0:T(8,128)S(1)} %pad_maximum_fusion.10), channel_id=1, source_target_pairs={{1,0},{2,1},{3,2},{4,3},{5,4},{6,5},{7,6},{9,8},{10,9},{11,10},{12... | collective-permute-start | bytes 73736 | tf_op jit(solution)/shard_map/ppermute | solution.py:19
  238.9 5.2 collective-permute-start.14
  402.4 6.2 %collective-permute-start.17 = (f32[1,1,32,64]{3,2,1,0:T(8,128)S(1)}, f32[1,1,32,64]{3,2,1,0:T(8,128)S(1)}, u32[]{:S(2)}, u32[]{:S(2)}) collective-permute-start(f32[1,1,32,64]{3,2,1,0:T(8,128)S(1)} %bitcast.109), channel_id=1, source_target_pairs={{8,0},{16,8},{24,16},{32,24},{40,32},{48,40},{56,48},{64,56},{72,6... | collective-permute-start | bytes 24584 | tf_op jit(solution)/shard_map/ppermute | solution.py:19
  406.6 7.8 %collective-permute-start.16 = (f32[1,1,32,64]{3,2,1,0:T(8,128)S(1)}, f32[1,1,32,64]{3,2,1,0:T(8,128)S(1)}, u32[]{:S(2)}, u32[]{:S(2)}) collective-permute-start(f32[1,1,32,64]{3,2,1,0:T(8,128)S(1)} %bitcast.110), channel_id=1, source_target_pairs={{0,8},{8,16},{16,24},{24,32},{32,40},{40,48},{48,56},{56,64},{64,7... | collective-permute-start | bytes 24584 | tf_op jit(solution)/shard_map/ppermute | solution.py:17
  414.5 5.9 %collective-permute-start.19 = (f32[3,1,32,64]{3,2,1,0:T(8,128)S(1)}, f32[3,1,32,64]{3,2,1,0:T(8,128)S(1)}, u32[]{:S(2)}, u32[]{:S(2)}) collective-permute-start(f32[3,1,32,64]{3,2,1,0:T(8,128)S(1)} %pad_maximum_fusion.11), channel_id=1, source_target_pairs={{1,0},{2,1},{3,2},{4,3},{5,4},{6,5},{7,6},{9,8},{10,9},{11,10},{12... | collective-permute-start | bytes 73736 | tf_op jit(solution)/shard_map/ppermute | solution.py:19
  421.8 5.3 collective-permute-start.21
  423.7 7.8 %collective-permute-start.20 = (f32[1,1,32,64]{3,2,1,0:T(8,128)S(1)}, f32[1,1,32,64]{3,2,1,0:T(8,128)S(1)}, u32[]{:S(2)}, u32[]{:S(2)}) collective-permute-start(f32[1,1,32,64]{3,2,1,0:T(8,128)S(1)} %convolution_bitcast_fusion), channel_id=1, source_target_pairs={{0,8},{8,16},{16,24},{24,32},{32,40},{40,48},{48,56},{56,64},{64,7... | collective-permute-start | bytes 24584 | tf_op jit(solution)/shard_map/ppermute | solution.py:17
  431.6 7.3 %collective-permute-start.23 = (f32[3,1,32,64]{3,2,1,0:T(8,128)S(1)}, f32[3,1,32,64]{3,2,1,0:T(8,128)S(1)}, u32[]{:S(2)}, u32[]{:S(2)}) collective-permute-start(f32[3,1,32,64]{3,2,1,0:T(8,128)S(1)} %pad_maximum_fusion.12), channel_id=1, source_target_pairs={{1,0},{2,1},{3,2},{4,3},{5,4},{6,5},{7,6},{9,8},{10,9},{11,10},{12... | collective-permute-start | bytes 73736 | tf_op jit(solution)/shard_map/ppermute | solution.py:19
  434.8 5.2 collective-permute-start.22
  523.5 5.6 %collective-permute-start.25 = (f32[1,1,32,64]{3,2,1,0:T(8,128)S(1)}, f32[1,1,32,64]{3,2,1,0:T(8,128)S(1)}, u32[]{:S(2)}, u32[]{:S(2)}) collective-permute-start(f32[1,1,32,64]{3,2,1,0:T(8,128)S(1)} %bitcast.105), channel_id=1, source_target_pairs={{8,0},{16,8},{24,16},{32,24},{40,32},{48,40},{56,48},{64,56},{72,6... | collective-permute-start | bytes 24584 | tf_op jit(solution)/shard_map/ppermute | solution.py:19
  527.2 7.8 %collective-permute-start.24 = (f32[1,1,32,64]{3,2,1,0:T(8,128)S(1)}, f32[1,1,32,64]{3,2,1,0:T(8,128)S(1)}, u32[]{:S(2)}, u32[]{:S(2)}) collective-permute-start(f32[1,1,32,64]{3,2,1,0:T(8,128)S(1)} %bitcast.106), channel_id=1, source_target_pairs={{0,8},{8,16},{16,24},{24,32},{32,40},{40,48},{48,56},{56,64},{64,7... | collective-permute-start | bytes 24584 | tf_op jit(solution)/shard_map/ppermute | solution.py:17
  535.0 7.7 %collective-permute-start.27 = (f32[3,1,32,64]{3,2,1,0:T(8,128)S(1)}, f32[3,1,32,64]{3,2,1,0:T(8,128)S(1)}, u32[]{:S(2)}, u32[]{:S(2)}) collective-permute-start(f32[3,1,32,64]{3,2,1,0:T(8,128)S(1)} %pad_maximum_fusion.13), channel_id=1, source_target_pairs={{1,0},{2,1},{3,2},{4,3},{5,4},{6,5},{7,6},{9,8},{10,9},{11,10},{12... | collective-permute-start | bytes 73736 | tf_op jit(solution)/shard_map/ppermute | solution.py:19
  (12 other events, 443.5 us)
where the time goes:
time: 563 us; the launch traced here: 561 us
  blocking collectives  381 us (68%)
  starting transfers between devices  87.6 us (16%)
  waiting for transfers between devices  43.8 us (8%)
  matrix products  32 us (6%)
  between operations  7.94 us (1%)
    psum x3, blocking collectives, squares(): return lax.psum(jnp.sum(values * values), ('gx', 'gy'))  221 us
    psum x2, blocking collectives, per_device(): alpha = norm_now / lax.psum(jnp.sum(direction * image), ('gx', 'gy'))  146 us
    ppermute x14, starting transfers between devices, with_halo(): lax.ppermute(head, axis, [((i + 1) % count, i) for i in range(ends)])  45.9 us
    ppermute x14, waiting for transfers between devices, with_halo(): lax.ppermute(tail, axis, [(i, (i + 1) % count) for i in range(ends)])  43.8 us
    ppermute x14, starting transfers between devices, with_halo(): lax.ppermute(tail, axis, [(i, (i + 1) % count) for i in range(ends)])  41.7 us
    dot_general x4, matrix products, coefficient(): jnp.einsum('bfv,bv->bf', features, field, precision=lax.Precision.HIGHEST)  22 us
    all_gather x1, blocking collectives, per_device(): slab_rows = lax.all_gather(surface, 'gy', axis=0, tiled=True)  13.1 us
  transfers between devices with their start and end apart: 28, of which 14 were waited for; matrix products, arithmetic and copies ran while one was open for 0% of the time, Pallas kernels for 0%

commit v1 on v0

--- a/solution.py
+++ b/solution.py
@@ -78,7 +78,12 @@
         direction = residual + norm_next / norm_now * direction
         norm_now = norm_next
     surface = first_sum(coefficient(features, solution_field))
-    slab_rows = lax.all_gather(surface, "gy", axis=0, tiled=True)
+    ring = [surface]
+    for hop in range(7):
+        ring.append(lax.ppermute(ring[-1], "gy", [(dev, (dev + 1) % 8) for dev in range(8)]))
+    slab_rows = jnp.roll(
+        jnp.concatenate(ring[::-1], axis=0), (lax.axis_index("gy") + 1) * ring[0].shape[0], axis=0
+    )
     local_ids = vertex_bricks - row_index * across * nrows
     picked = jnp.take(slab_rows, local_ids, axis=0)
     vertex_values = jnp.sum(vertex_features * picked.T, axis=0)

time: 563 us -> 579 us (1.028)
  starting transfers between devices: 87.6 us -> 101 us
  blocking collectives: 381 us -> 368 us
  waiting for transfers between devices: 43.8 us -> 56.5 us
    all_gather x1 -> x0, blocking collectives: 13.1 us -> none  [per_device(): slab_rows = lax.all_gather(surface, 'gy', axis=0, tiled=True)]
    ppermute x0 -> x7, starting transfers between devices: none -> 12.9 us  [per_device(): lax.ppermute(ring[-1], 'gy', [(dev, (dev + 1) % 8) for dev in range(8)])]
    ppermute x0 -> x7, waiting for transfers between devices: none -> 12.5 us  [per_device(): lax.ppermute(ring[-1], 'gy', [(dev, (dev + 1) % 8) for dev in range(8)])]
  transfers between devices with their start and end apart: 28 -> 35, of which waited for: 14 -> 21; matrix products, arithmetic and copies ran while one was open for 0% -> 0% of each run, Pallas kernels for 0% -> 0%
where the time goes in v1:
time: 579 us; the launch traced here: 573 us
  blocking collectives  368 us (64%)
  starting transfers between devices  101 us (17%)
  waiting for transfers between devices  56.5 us (10%)
  matrix products  32 us (6%)
  between operations  8.05 us (1%)
    psum x3, blocking collectives, squares(): return lax.psum(jnp.sum(values * values), ('gx', 'gy'))  221 us
    psum x2, blocking collectives, per_device(): alpha = norm_now / lax.psum(jnp.sum(direction * image), ('gx', 'gy'))  146 us
    ppermute x14, starting transfers between devices, with_halo(): lax.ppermute(head, axis, [((i + 1) % count, i) for i in range(ends)])  45.9 us
    ppermute x14, waiting for transfers between devices, with_halo(): lax.ppermute(tail, axis, [(i, (i + 1) % count) for i in range(ends)])  44 us
    ppermute x14, starting transfers between devices, with_halo(): lax.ppermute(tail, axis, [(i, (i + 1) % count) for i in range(ends)])  41.7 us
    dot_general x4, matrix products, coefficient(): jnp.einsum('bfv,bv->bf', features, field, precision=lax.Precision.HIGHEST)  22 us
    ppermute x7, starting transfers between devices, per_device(): lax.ppermute(ring[-1], 'gy', [(dev, (dev + 1) % 8) for dev in range(8)])  12.9 us
    ppermute x7, waiting for transfers between devices, per_device(): lax.ppermute(ring[-1], 'gy', [(dev, (dev + 1) % 8) for dev in range(8)])  12.5 us
  transfers between devices with their start and end apart: 35, of which 21 were waited for; matrix products, arithmetic and copies ran while one was open for 0% of the time, Pallas kernels for 0%

profile of v1, /device:TPU:129, one launch (start us, length us, event | category | flops | bytes accessed | tf_op | source)
XLA Modules:
  0.0 573.4 jit_solution(7082600023786779808)
XLA Ops:
  0.7 5.8 %fusion.8 = f32[32,1,64]{2,1,0:T(1,128)S(1)} fusion(f32[32,64,512]{2,1,0:T(8,128)} %param.8, f32[32,512,1]{1,0,2:T(8,128)} %bitcast.92), kind=kOutput, calls=%fused_computation.25 | convolution fusion | flops 12582912 | bytes 4268032 | tf_op jit(solution)/shard_map/bfv,bv->bf/dot_general | solution.py:27
  12.7 5.6 collective-permute-done
  18.2 4.0 collective-permute-start.3
  32.1 4.4 collective-permute-done.4
  38.6 5.2 collective-permute-start.6
  45.2 4.3 fusion.25
  50.2 74.5 %all-reduce = (f32[]{:T(128)}, f32[]{:T(128)}) all-reduce(f32[]{:T(128)} %get-tuple-element.4, f32[]{:T(128)} %get-tuple-element.3), channel_id=1, replica_groups=mesh['gx'=32,'gy'=8] {'gx','gy'}, use_global_device_ids=true, to_apply=%region_1.2 | all-reduce | flops 2 | bytes 16 | tf_op jit(solution)/shard_map/psum | solution.py:31
  126.7 73.5 %psum.44 = f32[]{:T(128)} all-reduce(f32[]{:T(128)} %get-tuple-element.9), channel_id=1, replica_groups=mesh['gx'=32,'gy'=8] {'gx','gy'}, use_global_device_ids=true, to_apply=%region_6.7 | all-reduce | flops 1 | bytes 8 | tf_op jit(solution)/shard_map/psum | solution.py:31
  201.5 5.4 fusion.6
  212.7 5.9 %collective-permute-done.8 = f32[1,1,32,64]{3,2,1,0:T(8,128)S(1)} collective-permute-done((f32[1,1,32,64]{3,2,1,0:T(8,128)S(1)}, f32[1,1,32,64]{3,2,1,0:T(8,128)S(1)}, u32[]{:S(2)}, u32[]{:S(2)}) %collective-permute-start.8) | collective-permute-done | bytes 8224 | tf_op jit(solution)/shard_map/ppermute | solution.py:17
  218.6 4.0 collective-permute-start.11
  231.3 4.4 collective-permute-done.12
  238.9 4.3 collective-permute-start.14
  247.1 73.2 %psum.45 = f32[]{:T(128)} all-reduce(f32[]{:T(128)} %multiply_reduce_fusion.2), channel_id=1, replica_groups=mesh['gx'=32,'gy'=8] {'gx','gy'}, use_global_device_ids=true, to_apply=%region_8.9 | all-reduce | flops 1 | bytes 8 | tf_op jit(solution)/shard_map/psum | solution.py:74
  322.3 73.3 %psum.46 = f32[]{:T(128)} all-reduce(f32[]{:T(128)} %get-tuple-element.7), channel_id=1, replica_groups=mesh['gx'=32,'gy'=8] {'gx','gy'}, use_global_device_ids=true, to_apply=%region_10.11 | all-reduce | flops 1 | bytes 8 | tf_op jit(solution)/shard_map/psum | solution.py:31
  397.0 5.4 fusion.4
  402.4 4.2 collective-permute-start.17
  408.6 5.9 %collective-permute-done.16 = f32[1,1,32,64]{3,2,1,0:T(8,128)S(1)} collective-permute-done((f32[1,1,32,64]{3,2,1,0:T(8,128)S(1)}, f32[1,1,32,64]{3,2,1,0:T(8,128)S(1)}, u32[]{:S(2)}, u32[]{:S(2)}) %collective-permute-start.16) | collective-permute-done | bytes 8224 | tf_op jit(solution)/shard_map/ppermute | solution.py:17
  427.1 4.4 collective-permute-done.20
  434.8 4.1 collective-permute-start.22
  443.0 73.2 %psum.47 = f32[]{:T(128)} all-reduce(f32[]{:T(128)} %multiply_reduce_fusion), channel_id=1, replica_groups=mesh['gx'=32,'gy'=8] {'gx','gy'}, use_global_device_ids=true, to_apply=%region_12.13 | all-reduce | flops 1 | bytes 8 | tf_op jit(solution)/shard_map/psum | solution.py:74
  518.2 5.3 fusion.2
  529.1 5.9 %collective-permute-done.24 = f32[1,1,32,64]{3,2,1,0:T(8,128)S(1)} collective-permute-done((f32[1,1,32,64]{3,2,1,0:T(8,128)S(1)}, f32[1,1,32,64]{3,2,1,0:T(8,128)S(1)}, u32[]{:S(2)}, u32[]{:S(2)}) %collective-permute-start.24) | collective-permute-done | bytes 8224 | tf_op jit(solution)/shard_map/ppermute | solution.py:17
  565.4 4.1 collective-permute-done.34
  (130 shorter events, 105.1 us)
Async XLA Ops:
  6.5 6.2 %collective-permute-start.1 = (f32[1,1,32,64]{3,2,1,0:T(8,128)S(1)}, f32[1,1,32,64]{3,2,1,0:T(8,128)S(1)}, u32[]{:S(2)}, u32[]{:S(2)}) collective-permute-start(f32[1,1,32,64]{3,2,1,0:T(8,128)S(1)} %bitcast.101), channel_id=1, source_target_pairs={{8,0},{16,8},{24,16},{32,24},{40,32},{48,40},{56,48},{64,56},{72,6... | collective-permute-start | bytes 24584 | tf_op jit(solution)/shard_map/ppermute | solution.py:19
  10.4 7.8 %collective-permute-start = (f32[1,1,32,64]{3,2,1,0:T(8,128)S(1)}, f32[1,1,32,64]{3,2,1,0:T(8,128)S(1)}, u32[]{:S(2)}, u32[]{:S(2)}) collective-permute-start(f32[1,1,32,64]{3,2,1,0:T(8,128)S(1)} %bitcast.102), channel_id=1, source_target_pairs={{0,8},{8,16},{16,24},{24,32},{32,40},{40,48},{48,56},{56,64},{64,7... | collective-permute-start | bytes 24584 | tf_op jit(solution)/shard_map/ppermute | solution.py:17
  18.2 7.4 %collective-permute-start.3 = (f32[3,1,32,64]{3,2,1,0:T(8,128)S(1)}, f32[3,1,32,64]{3,2,1,0:T(8,128)S(1)}, u32[]{:S(2)}, u32[]{:S(2)}) collective-permute-start(f32[3,1,32,64]{3,2,1,0:T(8,128)S(1)} %pad_maximum_fusion.7), channel_id=1, source_target_pairs={{1,0},{2,1},{3,2},{4,3},{5,4},{6,5},{7,6},{9,8},{10,9},{11,10},{12... | collective-permute-start | bytes 73736 | tf_op jit(solution)/shard_map/ppermute | solution.py:19
  26.8 5.3 collective-permute-start.5
  28.7 7.8 %collective-permute-start.4 = (f32[1,1,32,64]{3,2,1,0:T(8,128)S(1)}, f32[1,1,32,64]{3,2,1,0:T(8,128)S(1)}, u32[]{:S(2)}, u32[]{:S(2)}) collective-permute-start(f32[1,1,32,64]{3,2,1,0:T(8,128)S(1)} %convolution_bitcast_fusion.2), channel_id=1, source_target_pairs={{0,8},{8,16},{16,24},{24,32},{32,40},{40,48},{48,56},{56,64},{64,7... | collective-permute-start | bytes 24584 | tf_op jit(solution)/shard_map/ppermute | solution.py:17
  36.5 7.3 %collective-permute-start.7 = (f32[3,1,32,64]{3,2,1,0:T(8,128)S(1)}, f32[3,1,32,64]{3,2,1,0:T(8,128)S(1)}, u32[]{:S(2)}, u32[]{:S(2)}) collective-permute-start(f32[3,1,32,64]{3,2,1,0:T(8,128)S(1)} %pad_maximum_fusion.8), channel_id=1, source_target_pairs={{1,0},{2,1},{3,2},{4,3},{5,4},{6,5},{7,6},{9,8},{10,9},{11,10},{12... | collective-permute-start | bytes 73736 | tf_op jit(solution)/shard_map/ppermute | solution.py:19
  38.6 6.4 %collective-permute-start.6 = (f32[3,1,32,64]{3,2,1,0:T(8,128)S(1)}, f32[3,1,32,64]{3,2,1,0:T(8,128)S(1)}, u32[]{:S(2)}, u32[]{:S(2)}) collective-permute-start(f32[3,1,32,64]{3,2,1,0:T(8,128)S(1)} %pad_maximum_fusion.8), channel_id=1, source_target_pairs={{0,1},{1,2},{2,3},{3,4},{4,5},{5,6},{6,7},{8,9},{9,10},{10,11},{11... | collective-permute-start | bytes 73736 | tf_op jit(solution)/shard_map/ppermute | solution.py:17
  206.9 5.8 %collective-permute-start.9 = (f32[1,1,32,64]{3,2,1,0:T(8,128)S(1)}, f32[1,1,32,64]{3,2,1,0:T(8,128)S(1)}, u32[]{:S(2)}, u32[]{:S(2)}) collective-permute-start(f32[1,1,32,64]{3,2,1,0:T(8,128)S(1)} %bitcast.109), channel_id=1, source_target_pairs={{8,0},{16,8},{24,16},{32,24},{40,32},{48,40},{56,48},{64,56},{72,6... | collective-permute-start | bytes 24584 | tf_op jit(solution)/shard_map/ppermute | solution.py:19
  210.8 7.8 %collective-permute-start.8 = (f32[1,1,32,64]{3,2,1,0:T(8,128)S(1)}, f32[1,1,32,64]{3,2,1,0:T(8,128)S(1)}, u32[]{:S(2)}, u32[]{:S(2)}) collective-permute-start(f32[1,1,32,64]{3,2,1,0:T(8,128)S(1)} %bitcast.110), channel_id=1, source_target_pairs={{0,8},{8,16},{16,24},{24,32},{32,40},{40,48},{48,56},{56,64},{64,7... | collective-permute-start | bytes 24584 | tf_op jit(solution)/shard_map/ppermute | solution.py:17
  218.6 5.9 %collective-permute-start.11 = (f32[3,1,32,64]{3,2,1,0:T(8,128)S(1)}, f32[3,1,32,64]{3,2,1,0:T(8,128)S(1)}, u32[]{:S(2)}, u32[]{:S(2)}) collective-permute-start(f32[3,1,32,64]{3,2,1,0:T(8,128)S(1)} %pad_maximum_fusion.9), channel_id=1, source_target_pairs={{1,0},{2,1},{3,2},{4,3},{5,4},{6,5},{7,6},{9,8},{10,9},{11,10},{12... | collective-permute-start | bytes 73736 | tf_op jit(solution)/shard_map/ppermute | solution.py:19
  226.0 5.3 collective-permute-start.13
  227.9 7.8 %collective-permute-start.12 = (f32[1,1,32,64]{3,2,1,0:T(8,128)S(1)}, f32[1,1,32,64]{3,2,1,0:T(8,128)S(1)}, u32[]{:S(2)}, u32[]{:S(2)}) collective-permute-start(f32[1,1,32,64]{3,2,1,0:T(8,128)S(1)} %convolution_bitcast_fusion.1), channel_id=1, source_target_pairs={{0,8},{8,16},{16,24},{24,32},{32,40},{40,48},{48,56},{56,64},{64,7... | collective-permute-start | bytes 24584 | tf_op jit(solution)/shard_map/ppermute | solution.py:17
  235.7 7.5 %collective-permute-start.15 = (f32[3,1,32,64]{3,2,1,0:T(8,128)S(1)}, f32[3,1,32,64]{3,2,1,0:T(8,128)S(1)}, u32[]{:S(2)}, u32[]{:S(2)}) collective-permute-start(f32[3,1,32,64]{3,2,1,0:T(8,128)S(1)} %pad_maximum_fusion.10), channel_id=1, source_target_pairs={{1,0},{2,1},{3,2},{4,3},{5,4},{6,5},{7,6},{9,8},{10,9},{11,10},{12... | collective-permute-start | bytes 73736 | tf_op jit(solution)/shard_map/ppermute | solution.py:19
  238.9 5.2 collective-permute-start.14
  402.4 6.2 %collective-permute-start.17 = (f32[1,1,32,64]{3,2,1,0:T(8,128)S(1)}, f32[1,1,32,64]{3,2,1,0:T(8,128)S(1)}, u32[]{:S(2)}, u32[]{:S(2)}) collective-permute-start(f32[1,1,32,64]{3,2,1,0:T(8,128)S(1)} %bitcast.105), channel_id=1, source_target_pairs={{8,0},{16,8},{24,16},{32,24},{40,32},{48,40},{56,48},{64,56},{72,6... | collective-permute-start | bytes 24584 | tf_op jit(solution)/shard_map/ppermute | solution.py:19
  406.6 7.8 %collective-permute-start.16 = (f32[1,1,32,64]{3,2,1,0:T(8,128)S(1)}, f32[1,1,32,64]{3,2,1,0:T(8,128)S(1)}, u32[]{:S(2)}, u32[]{:S(2)}) collective-permute-start(f32[1,1,32,64]{3,2,1,0:T(8,128)S(1)} %bitcast.106), channel_id=1, source_target_pairs={{0,8},{8,16},{16,24},{24,32},{32,40},{40,48},{48,56},{56,64},{64,7... | collective-permute-start | bytes 24584 | tf_op jit(solution)/shard_map/ppermute | solution.py:17
  414.5 5.9 %collective-permute-start.19 = (f32[3,1,32,64]{3,2,1,0:T(8,128)S(1)}, f32[3,1,32,64]{3,2,1,0:T(8,128)S(1)}, u32[]{:S(2)}, u32[]{:S(2)}) collective-permute-start(f32[3,1,32,64]{3,2,1,0:T(8,128)S(1)} %pad_maximum_fusion.11), channel_id=1, source_target_pairs={{1,0},{2,1},{3,2},{4,3},{5,4},{6,5},{7,6},{9,8},{10,9},{11,10},{12... | collective-permute-start | bytes 73736 | tf_op jit(solution)/shard_map/ppermute | solution.py:19
  421.8 5.3 collective-permute-start.21
  423.7 7.8 %collective-permute-start.20 = (f32[1,1,32,64]{3,2,1,0:T(8,128)S(1)}, f32[1,1,32,64]{3,2,1,0:T(8,128)S(1)}, u32[]{:S(2)}, u32[]{:S(2)}) collective-permute-start(f32[1,1,32,64]{3,2,1,0:T(8,128)S(1)} %convolution_bitcast_fusion), channel_id=1, source_target_pairs={{0,8},{8,16},{16,24},{24,32},{32,40},{40,48},{48,56},{56,64},{64,7... | collective-permute-start | bytes 24584 | tf_op jit(solution)/shard_map/ppermute | solution.py:17
  431.6 7.3 %collective-permute-start.23 = (f32[3,1,32,64]{3,2,1,0:T(8,128)S(1)}, f32[3,1,32,64]{3,2,1,0:T(8,128)S(1)}, u32[]{:S(2)}, u32[]{:S(2)}) collective-permute-start(f32[3,1,32,64]{3,2,1,0:T(8,128)S(1)} %pad_maximum_fusion.12), channel_id=1, source_target_pairs={{1,0},{2,1},{3,2},{4,3},{5,4},{6,5},{7,6},{9,8},{10,9},{11,10},{12... | collective-permute-start | bytes 73736 | tf_op jit(solution)/shard_map/ppermute | solution.py:19
  434.8 5.2 collective-permute-start.22
  523.5 5.6 collective-permute-start.25
  527.2 7.8 %collective-permute-start.24 = (f32[1,1,32,64]{3,2,1,0:T(8,128)S(1)}, f32[1,1,32,64]{3,2,1,0:T(8,128)S(1)}, u32[]{:S(2)}, u32[]{:S(2)}) collective-permute-start(f32[1,1,32,64]{3,2,1,0:T(8,128)S(1)} %bitcast.114), channel_id=1, source_target_pairs={{0,8},{8,16},{16,24},{24,32},{32,40},{40,48},{48,56},{56,64},{64,7... | collective-permute-start | bytes 24584 | tf_op jit(solution)/shard_map/ppermute | solution.py:17
  535.0 7.5 %collective-permute-start.27 = (f32[3,1,32,64]{3,2,1,0:T(8,128)S(1)}, f32[3,1,32,64]{3,2,1,0:T(8,128)S(1)}, u32[]{:S(2)}, u32[]{:S(2)}) collective-permute-start(f32[3,1,32,64]{3,2,1,0:T(8,128)S(1)} %pad_maximum_fusion.13), channel_id=1, source_target_pairs={{1,0},{2,1},{3,2},{4,3},{5,4},{6,5},{7,6},{9,8},{10,9},{11,10},{12... | collective-permute-start | bytes 73736 | tf_op jit(solution)/shard_map/ppermute | solution.py:19
  (19 other events, 537.4 us)
